TPU v7x, 512 devices: a whole 4x4x16 slice. The times are simulated.
512 devices in a mesh: dom: 64 (over z, y), src: 4 (over x), rel: 2 (over core).
Axes of the slice: x: 4, y: 4, z: 16, core: 2. Of those that a mesh axis runs over, the one named last changes fastest.
Arguments:
- source_feats: bfloat16 [131072, 256], P(('dom', 'src', 'rel')), may hold values from -6 to 6
- rel_weight: bfloat16 [12, 256, 256], P('rel'), may hold values from -0.375 to 0.375
- halo_pick: int32 [64, 4, 2, 64], P('dom', 'src', 'rel'), may hold values from 0 to 1
- entry_index: int32 [64, 4, 2, 3, 64], P('dom', 'src', 'rel'), may hold values from 0 to 63, as said below
- entry_count: int32 [64, 4, 2], P('dom', 'src', 'rel'), may hold values from 1 to 64, as said below
- entry_values: bfloat16 [64, 4, 2, 64, 128, 128], P('dom', 'src', 'rel'), may hold values from -0.125 to 0.125
- cotangent: bfloat16 [131072, 256], P(('dom', 'src', 'rel')), may hold values from -0.0546875 to 0.0546875
Outputs:
- out_feats: bfloat16 [131072, 256], P(('dom', 'src', 'rel'))
- grad_rel: float32 [12, 256, 256], P('rel')
Inputs may be any that keep to these rules, and one draw needn't show every extreme that they name: `entry_index`: row 0 of an entry is a target block below 16, row 1 a partition below 64, row 2 a relation below 6. Over all 64 entries of one (p,s,g), every partition is named 64 // 64 times or once more. `entry_count`: live entries come first; some (p,s,g) has all 64 entries live in every draw.
All inputs are finite; a program needn't handle non-finite values.
Results may differ from a plain program's by a relative error of at most 0.0057.
Values may be sent and summed in bfloat16 or wider, within the bound.
A program may use at most 64 MiB of HBM per device.

v0:
```python
import jax
import jax.numpy as jnp
from jax import lax
from jax.sharding import PartitionSpec as P


def silu_slope(pre_values):
    logistic = jax.nn.sigmoid(pre_values)
    return logistic * (1.0 + pre_values * (1.0 - logistic))


def local(source_feats, rel_weight, halo_pick, entry_index, entry_count, entry_values, cotangent):
    partitions = lax.axis_size("dom")
    tile_rows = entry_values.shape[-1]
    features = source_feats.shape[1]
    chosen = halo_pick.reshape(-1)
    everyone = lax.all_gather(source_feats, "dom", axis=0, tiled=True)
    everyone = everyone.reshape(partitions, -1, tile_rows, features)
    halo_blocks = everyone[jnp.arange(partitions, dtype=jnp.int32), chosen]
    own_rows = cotangent.shape[0]
    tgt_blocks = own_rows * lax.axis_size("src") * lax.axis_size("rel") // tile_rows
    rel_local = rel_weight.shape[0]
    entry_table = entry_index.reshape(3, -1)
    slot_total = entry_table.shape[1]
    values = entry_values.reshape(-1, tile_rows, tile_rows)
    picked = halo_blocks[entry_table[1]]
    messages = jnp.einsum("eij,ejd->eid", values, picked, preferred_element_type=jnp.float32)
    live_mask = jnp.arange(slot_total, dtype=jnp.int32) < entry_count.reshape(())
    target_slot = entry_table[2] * tgt_blocks + entry_table[0]
    slot_numbers = jnp.arange(rel_local * tgt_blocks, dtype=jnp.int32)
    placement = ((slot_numbers[:, None] == target_slot[None, :]) & live_mask[None, :]).astype(
        jnp.float32
    )
    totals = jnp.einsum(
        "se,eid->sid",
        placement,
        messages,
        precision=lax.Precision.HIGHEST,
        preferred_element_type=jnp.float32,
    )
    relation_terms = totals.astype(jnp.bfloat16).reshape(
        rel_local, tgt_blocks * tile_rows, features
    )
    summed = lax.psum_scatter(
        jnp.einsum("rtd,rde->te", relation_terms, rel_weight, preferred_element_type=jnp.float32),
        ("src", "rel"),
        scatter_dimension=0,
        tiled=True,
    )
    out_feats = jax.nn.silu(summed).astype(jnp.bfloat16)
    local_grad = (cotangent.astype(jnp.float32) * silu_slope(summed)).astype(jnp.bfloat16)
    grad_rows = lax.all_gather(local_grad, ("src", "rel"), axis=0, tiled=True)
    weight_terms = jnp.einsum(
        "rtd,te->rde", relation_terms, grad_rows, preferred_element_type=jnp.float32
    )
    grad_rel = lax.psum(weight_terms, ("dom", "src"))
    return (out_feats, grad_rel)


def solution(mesh):
    return jax.shard_map(
        local,
        mesh=mesh,
        in_specs=(
            P(("dom", "src", "rel"), None),
            P("rel", None, None),
            P("dom", "src", "rel", None),
            P("dom", "src", "rel", None, None),
            P("dom", "src", "rel"),
            P("dom", "src", "rel", None, None, None),
            P(("dom", "src", "rel"), None),
        ),
        out_specs=(P(("dom", "src", "rel"), None), P("rel", None, None)),
        check_vma=False,
    )
```

profile of v0, /device:TPU:2, one launch (start us, length us, event | category | flops | bytes accessed | tf_op | source)
XLA Modules:
  0.0 711.4 jit_solution(15321850771566686382)
XLA Ops:
  7.2 0.0 all-gather.3.cloned.1.call-start
  7.2 0.7 all-gather.3.cloned.1.call-update
  7.9 0.0 reduce-scatter.2.cloned.1.call-start
  8.6 0.7 fusion.17
  9.3 0.7 add_bitcast_fusion
  10.0 0.7 fusion.18
  10.6 160.9 %all-gather.3.cloned.1.call-done = bf16[16384,256]{1,0:T(8,128)(2,1)} async-done(((bf16[256,256]{1,0:T(8,128)(2,1)}), bf16[16384,256]{1,0:T(8,128)(2,1)}) %all-gather.3.cloned.1.call-update) | async-done | bytes 8388624 | tf_op jit(solution)/shard_map/all_gather | solution.py:17
  171.5 6.2 gather_fusion
  177.7 4.9 gather_fusion.1
  182.6 6.7 fusion.5
  189.3 9.2 %copy.12 = f32[64,256,128]{1,0,2:T(8,128)} copy(f32[64,256,128]{2,1,0:T(8,128)} %fusion.5) | data formatting | bytes 16777216 | tf_op jit(solution)/shard_map/eij,ejd->eid/dot_general | solution.py:27
  198.5 8.4 %fusion.2 = bf16[96,128,256]{2,0,1:T(8,128)(2,1)S(1)} fusion(f32[64,256,128]{1,0,2:T(8,128)} %copy.12, s32[64]{0:T(128)S(1)} %add_bitcast_fusion, pred[64]{0:T(512)(128)(4,1)S(1)} %iota_compare_fusion.1), kind=kOutput, calls=%fused_computation.4 | convolution fusion | flops 2419077120 | bytes 14680384 | tf_op jit(solution)/shard_map/se,eid->sid/dot_general | solution.py:34
  207.0 3.7 copy.10
  210.6 2.6 copy-done.1
  213.3 3.3 convolution_bitcast_fusion
  216.6 0.0 all-gather.5.cloned.1.call-start
  216.6 33.4 %reduce-scatter.2.cloned.1.call-done = f32[256,256]{1,0:T(8,128)} async-done(((f32[2048,256]{1,0:T(8,128)}), f32[256,256]{1,0:T(8,128)}) %reduce-scatter.2.cloned.1.call-update) | async-done | bytes 262160 | tf_op jit(solution)/shard_map/reduce_scatter | solution.py:44
  250.0 1.8 multiply_convert_fusion
  251.7 0.0 all-gather.5.cloned.1.call-update
  251.8 0.0 all-reduce.2.cloned.1.call-start
  251.8 32.6 %all-gather.5.cloned.1.call-done = bf16[2048,256]{1,0:T(8,128)(2,1)} async-done(((bf16[256,256]{1,0:T(8,128)(2,1)}), bf16[2048,256]{1,0:T(8,128)(2,1)}) %all-gather.5.cloned.1.call-update) | async-done | bytes 1048592 | tf_op jit(solution)/shard_map/all_gather | solution.py:52
  284.4 6.0 fusion.7
  290.4 411.6 %all-reduce.2.cloned.1.call-done = f32[6,256,256]{2,1,0:T(8,128)} async-done(((f32[6,256,256]{2,1,0:T(8,128)}), f32[6,256,256]{2,1,0:T(8,128)}) %all-reduce.2.cloned.1.call-update) | async-done | bytes 1572880 | tf_op jit(solution)/shard_map/psum | solution.py:56
  702.1 2.7 copy.16
  (11 shorter events, 0.1 us)
Async XLA Ops:
  7.2 175.5 %copy-start = (bf16[1,1,1,64,128,128]{5,4,3,2,1,0:T(8,128)(2,1)S(1)}, bf16[1,1,1,64,128,128]{5,4,3,2,1,0:T(8,128)(2,1)}, u32[]{:S(2)}) copy-start(bf16[1,1,1,64,128,128]{5,4,3,2,1,0:T(8,128)(2,1)} %param.12) | copy-start | bytes 6291460
  7.2 164.4 %all-gather.3.cloned.1.call-start = ((), (), s32[]{:S(2)}) async-start(), calls=%async_computation.1 | async-start | bytes 8519680 | tf_op jit(solution)/shard_map/all_gather | solution.py:17
  7.9 242.1 %reduce-scatter.2.cloned.1.call-start = ((), (), s32[]{:S(2)}) async-start(), calls=%async_computation.2 | async-start | bytes 2359296 | tf_op jit(solution)/shard_map/reduce_scatter | solution.py:44
  207.0 6.3 copy-start.3
  210.6 2.7 copy-start.1
  213.3 36.7 %copy-start.2 = (bf16[256,256]{1,0:T(8,128)(2,1)S(1)}, bf16[256,256]{1,0:T(8,128)(2,1)}, u32[]{:S(2)}) copy-start(bf16[256,256]{1,0:T(8,128)(2,1)} %param.13) | copy-start | bytes 393220
  216.6 67.8 %all-gather.5.cloned.1.call-start = ((), (), s32[]{:S(2)}) async-start(), calls=%async_computation.3 | async-start | bytes 1179648 | tf_op jit(solution)/shard_map/all_gather | solution.py:52
  251.8 450.3 %all-reduce.2.cloned.1.call-start = ((), (), s32[]{:S(2)}) async-start(), calls=%async_computation.4 | async-start | bytes 3145728 | tf_op jit(solution)/shard_map/psum | solution.py:56
Sparse Core Ops, SparseCore 0:
  10.9 160.5 all-gather.2
  216.7 33.2 reduce-scatter.1
  252.7 31.6 all-gather.4
  290.6 411.4 all-reduce.1
where the time goes:
time: 712 us; the launch traced here: 711 us
  waiting for transfers between devices  639 us (90%)
  local copies, waits for them, and re-layouts  29.3 us (4%)
  matrix products  24.4 us (3%)
  between operations  14.5 us (2%)
    psum x1, waiting for transfers between devices, local(): grad_rel = lax.psum(weight_terms, ('dom', 'src'))  412 us
    all_gather x1, waiting for transfers between devices, local(): everyone = lax.all_gather(source_feats, 'dom', axis=0, tiled=True)  161 us
    reduce_scatter x1, waiting for transfers between devices, local(): lax.psum_scatter(jnp.einsum('rtd,rde->te', relation_terms, rel_weight, pr...  33.4 us
    all_gather x1, waiting for transfers between devices, local(): grad_rows = lax.all_gather(local_grad, ('src', 'rel'), axis=0, tiled=True)  32.6 us
  transfers between devices with their start and end apart: 4, of which 4 were waited for; matrix products, arithmetic and copies ran while one was open for 0% of the time, Pallas kernels for 0%

commit v1 on v0

--- a/solution.py
+++ b/solution.py
@@ -53,7 +53,7 @@
     weight_terms = jnp.einsum(
         "rtd,te->rde", relation_terms, grad_rows, preferred_element_type=jnp.float32
     )
-    grad_rel = lax.psum(weight_terms, ("dom", "src"))
+    grad_rel = lax.psum(lax.psum(weight_terms, "dom"), "src")
     return (out_feats, grad_rel)
 
 

time: 712 us -> 645 us (0.906)
  the two profiles are of different devices: /device:TPU:2 before, /device:TPU:1 now
where the time goes in v1:
time: 645 us; the launch traced here: 644 us
  waiting for transfers between devices  572 us (89%)
  local copies, waits for them, and re-layouts  29.3 us (5%)
  matrix products  24.4 us (4%)
  between operations  14.5 us (2%)
    psum x2, waiting for transfers between devices, local(): grad_rel = lax.psum(lax.psum(weight_terms, 'dom'), 'src')  342 us
    all_gather x1, waiting for transfers between devices, local(): everyone = lax.all_gather(source_feats, 'dom', axis=0, tiled=True)  154 us
    reduce_scatter x1, waiting for transfers between devices, local(): lax.psum_scatter(jnp.einsum('rtd,rde->te', relation_terms, rel_weight, pr...  42.6 us
    all_gather x1, waiting for transfers between devices, local(): grad_rows = lax.all_gather(local_grad, ('src', 'rel'), axis=0, tiled=True)  32.9 us
  transfers between devices with their start and end apart: 5, of which 5 were waited for; matrix products, arithmetic and copies ran while one was open for 0% of the time, Pallas kernels for 0%

profile of v1, /device:TPU:1, one launch (start us, length us, event | category | flops | bytes accessed | tf_op | source)
XLA Modules:
  0.0 644.1 jit_solution(10540853925808808199)
XLA Ops:
  7.2 0.7 all-gather.3.cloned.1.call-update
  7.9 0.0 reduce-scatter.2.cloned.1.call-start
  8.6 0.7 fusion.17
  9.3 0.7 add_bitcast_fusion
  10.0 0.7 fusion.18
  10.6 154.0 %all-gather.3.cloned.1.call-done = bf16[16384,256]{1,0:T(8,128)(2,1)} async-done(((bf16[256,256]{1,0:T(8,128)(2,1)}), bf16[16384,256]{1,0:T(8,128)(2,1)}) %all-gather.3.cloned.1.call-update) | async-done | bytes 8388624 | tf_op jit(solution)/shard_map/all_gather | solution.py:17
  164.6 6.2 gather_fusion
  170.8 4.9 gather_fusion.1
  175.7 6.7 %fusion.5 = f32[64,256,128]{2,1,0:T(8,128)} fusion(bf16[64,128,256]{2,1,0:T(8,128)(2,1)} %gather_fusion.1, bf16[1,1,1,64,128,128]{5,4,3,2,1,0:T(8,128)(2,1)S(1)} %copy-done), kind=kOutput, calls=%fused_computation.6 | convolution fusion | flops 536870912 | bytes 14680064 | tf_op jit(solution)/shard_map/eij,ejd->eid/dot_general | solution.py:27
  182.4 9.2 %copy.12 = f32[64,256,128]{1,0,2:T(8,128)} copy(f32[64,256,128]{2,1,0:T(8,128)} %fusion.5) | data formatting | bytes 16777216 | tf_op jit(solution)/shard_map/eij,ejd->eid/dot_general | solution.py:27
  191.6 8.4 %fusion.2 = bf16[96,128,256]{2,0,1:T(8,128)(2,1)S(1)} fusion(f32[64,256,128]{1,0,2:T(8,128)} %copy.12, s32[64]{0:T(128)S(1)} %add_bitcast_fusion, pred[64]{0:T(512)(128)(4,1)S(1)} %iota_compare_fusion.1), kind=kOutput, calls=%fused_computation.4 | convolution fusion | flops 2419077120 | bytes 14680384 | tf_op jit(solution)/shard_map/se,eid->sid/dot_general | solution.py:34
  200.1 3.7 copy.10
  203.7 2.6 copy-done.1
  206.4 3.3 convolution_bitcast_fusion
  209.7 0.0 all-gather.5.cloned.1.call-start
  209.7 42.6 %reduce-scatter.2.cloned.1.call-done = f32[256,256]{1,0:T(8,128)} async-done(((f32[2048,256]{1,0:T(8,128)}), f32[256,256]{1,0:T(8,128)}) %reduce-scatter.2.cloned.1.call-update) | async-done | bytes 262160 | tf_op jit(solution)/shard_map/reduce_scatter | solution.py:44
  252.3 1.8 multiply_convert_fusion
  254.1 0.0 all-reduce.3.cloned.1.call-start
  254.2 32.9 %all-gather.5.cloned.1.call-done = bf16[2048,256]{1,0:T(8,128)(2,1)} async-done(((bf16[256,256]{1,0:T(8,128)(2,1)}), bf16[2048,256]{1,0:T(8,128)(2,1)}) %all-gather.5.cloned.1.call-update) | async-done | bytes 1048592 | tf_op jit(solution)/shard_map/all_gather | solution.py:52
  287.1 6.0 fusion.7
  293.1 0.0 all-reduce.5.cloned.1.call-start
  293.2 268.8 %all-reduce.3.cloned.1.call-done = f32[6,256,256]{2,1,0:T(8,128)} async-done(((f32[6,256,256]{2,1,0:T(8,128)}), f32[6,256,256]{2,1,0:T(8,128)}) %all-reduce.3.cloned.1.call-update) | async-done | bytes 1572880 | tf_op jit(solution)/shard_map/psum | solution.py:56
  562.0 72.8 %all-reduce.5.cloned.1.call-done = f32[6,256,256]{2,1,0:T(8,128)} async-done(((f32[6,256,256]{2,1,0:T(8,128)}), f32[6,256,256]{2,1,0:T(8,128)}) %all-reduce.5.cloned.1.call-update) | async-done | bytes 1572880 | tf_op jit(solution)/shard_map/psum | solution.py:56
  634.9 2.7 copy.17
  (14 shorter events, 0.1 us)
Async XLA Ops:
  7.2 168.6 %copy-start = (bf16[1,1,1,64,128,128]{5,4,3,2,1,0:T(8,128)(2,1)S(1)}, bf16[1,1,1,64,128,128]{5,4,3,2,1,0:T(8,128)(2,1)}, u32[]{:S(2)}) copy-start(bf16[1,1,1,64,128,128]{5,4,3,2,1,0:T(8,128)(2,1)} %param.12) | copy-start | bytes 6291460
  7.2 157.5 %all-gather.3.cloned.1.call-start = ((), (), s32[]{:S(2)}) async-start(), calls=%async_computation.1 | async-start | bytes 8519680 | tf_op jit(solution)/shard_map/all_gather | solution.py:17
  7.9 244.4 %reduce-scatter.2.cloned.1.call-start = ((), (), s32[]{:S(2)}) async-start(), calls=%async_computation.2 | async-start | bytes 2359296 | tf_op jit(solution)/shard_map/reduce_scatter | solution.py:44
  200.0 6.3 copy-start.3
  203.7 2.7 copy-start.1
  206.4 46.0 %copy-start.2 = (bf16[256,256]{1,0:T(8,128)(2,1)S(1)}, bf16[256,256]{1,0:T(8,128)(2,1)}, u32[]{:S(2)}) copy-start(bf16[256,256]{1,0:T(8,128)(2,1)} %param.13) | copy-start | bytes 393220
  209.7 77.4 %all-gather.5.cloned.1.call-start = ((), (), s32[]{:S(2)}) async-start(), calls=%async_computation.3 | async-start | bytes 1179648 | tf_op jit(solution)/shard_map/all_gather | solution.py:52
  254.1 307.9 %all-reduce.3.cloned.1.call-start = ((), (), s32[]{:S(2)}) async-start(), calls=%async_computation.4 | async-start | bytes 3145728 | tf_op jit(solution)/shard_map/psum | solution.py:56
  293.1 341.7 %all-reduce.5.cloned.1.call-start = ((), (), s32[]{:S(2)}) async-start(), calls=%async_computation.5 | async-start | bytes 3145728 | tf_op jit(solution)/shard_map/psum | solution.py:56
Sparse Core Ops, SparseCore 0:
  10.9 153.6 all-gather.2
  209.8 42.5 reduce-scatter.1
  255.1 31.9 all-gather.4
  293.3 268.7 all-reduce.2
  564.2 70.5 all-reduce.4

commit v2 on v0

--- a/solution.py
+++ b/solution.py
@@ -14,7 +14,9 @@
     tile_rows = entry_values.shape[-1]
     features = source_feats.shape[1]
     chosen = halo_pick.reshape(-1)
-    everyone = lax.all_gather(source_feats, "dom", axis=0, tiled=True)
+    everyone = jnp.concatenate(
+        lax.all_to_all(jnp.stack([source_feats] * lax.axis_size("dom")), "dom", 0, 0), axis=0
+    )
     everyone = everyone.reshape(partitions, -1, tile_rows, features)
     halo_blocks = everyone[jnp.arange(partitions, dtype=jnp.int32), chosen]
     own_rows = cotangent.shape[0]

time: 712 us -> 938 us (1.32)
  waiting for transfers between devices: 639 us -> 843 us
  starting transfers between devices: 0.16 us -> 19.3 us
    all_to_all x0 -> x1, waiting for transfers between devices: none -> 369 us  [local(): lax.all_to_all(jnp.stack([source_feats] * lax.axis_size('dom')), 'dom', 0...]
    all_gather x1 -> x0, waiting for transfers between devices: 161 us -> none  [local(): everyone = lax.all_gather(source_feats, 'dom', axis=0, tiled=True)]
    all_to_all x0 -> x1, starting transfers between devices: none -> 19.1 us  [local(): lax.all_to_all(jnp.stack([source_feats] * lax.axis_size('dom')), 'dom', 0...]
where the time goes in v2:
time: 938 us
  waiting for transfers between devices  843 us (90%)
  local copies, waits for them, and re-layouts  34.7 us (4%)
  matrix products  24.4 us (3%)
  starting transfers between devices  19.3 us (2%)
  between operations  14.5 us (2%)
    psum x1, waiting for transfers between devices, local(): grad_rel = lax.psum(weight_terms, ('dom', 'src'))  412 us
    all_to_all x1, waiting for transfers between devices, local(): lax.all_to_all(jnp.stack([source_feats] * lax.axis_size('dom')), 'dom', 0...  369 us
    all_gather x1, waiting for transfers between devices, local(): grad_rows = lax.all_gather(local_grad, ('src', 'rel'), axis=0, tiled=True)  32.6 us
    reduce_scatter x1, waiting for transfers between devices, local(): lax.psum_scatter(jnp.einsum('rtd,rde->te', relation_terms, rel_weight, pr...  29.9 us
    all_to_all x1, starting transfers between devices, local(): lax.all_to_all(jnp.stack([source_feats] * lax.axis_size('dom')), 'dom', 0...  19.1 us
  transfers between devices with their start and end apart: 4, of which 4 were waited for; matrix products, arithmetic and copies ran while one was open for 0% of the time, Pallas kernels for 0%

profile of v2, /device:TPU:2, one launch (start us, length us, event | category | flops | bytes accessed | tf_op | source)
XLA Modules:
  0.0 937.9 jit_solution(7396073094082545487)
XLA Ops:
  7.2 0.0 copy-start
  7.2 5.3 stack.2
  12.5 19.1 %all-to-all-start = ((bf16[64,256,256]{2,1,0:T(8,128)(2,1)}), bf16[64,256,256]{2,1,0:T(8,128)(2,1)}, u32[]{:S(2)}, u32[]{:S(2)}) async-start(bf16[64,256,256]{2,1,0:T(8,128)(2,1)} %stack.2), calls=%async_computation | async-start | bytes 16777216 | tf_op jit(solution)/shard_map/all_to_all | solution.py:18
  31.6 0.0 reduce-scatter.2.cloned.1.call-start
  32.4 369.0 %all-to-all-done = bf16[64,256,256]{2,1,0:T(8,128)(2,1)} async-done(((bf16[64,256,256]{2,1,0:T(8,128)(2,1)}), bf16[64,256,256]{2,1,0:T(8,128)(2,1)}, u32[]{:S(2)}, u32[]{:S(2)}) %all-to-all-start) | async-done | bytes 8388640 | tf_op jit(solution)/shard_map/all_to_all | solution.py:18
  401.4 6.2 gather_fusion
  407.5 4.9 gather_fusion.1
  412.5 6.7 fusion.5
  419.2 9.3 copy.12
  428.4 8.5 fusion.2
  436.9 3.7 copy.10
  440.6 2.6 copy-done.1
  443.2 3.2 convolution_bitcast_fusion
  446.5 0.0 reduce-scatter.2.cloned.1.call-update
  446.5 0.0 all-gather.2.cloned.1.call-start
  446.5 29.9 %reduce-scatter.2.cloned.1.call-done = f32[256,256]{1,0:T(8,128)} async-done(((f32[2048,256]{1,0:T(8,128)}), f32[256,256]{1,0:T(8,128)}) %reduce-scatter.2.cloned.1.call-update) | async-done | bytes 262160 | tf_op jit(solution)/shard_map/reduce_scatter | solution.py:46
  476.4 1.8 multiply_convert_fusion
  478.2 0.0 all-gather.2.cloned.1.call-update
  478.2 0.0 all-reduce.2.cloned.1.call-start
  478.3 32.6 %all-gather.2.cloned.1.call-done = bf16[2048,256]{1,0:T(8,128)(2,1)} async-done(((bf16[256,256]{1,0:T(8,128)(2,1)}), bf16[2048,256]{1,0:T(8,128)(2,1)}) %all-gather.2.cloned.1.call-update) | async-done | bytes 1048592 | tf_op jit(solution)/shard_map/all_gather | solution.py:54
  510.9 6.0 fusion.7
  516.9 0.0 all-reduce.2.cloned.1.call-update
  516.9 411.6 %all-reduce.2.cloned.1.call-done = f32[6,256,256]{2,1,0:T(8,128)} async-done(((f32[6,256,256]{2,1,0:T(8,128)}), f32[6,256,256]{2,1,0:T(8,128)}) %all-reduce.2.cloned.1.call-update) | async-done | bytes 1572880 | tf_op jit(solution)/shard_map/psum | solution.py:58
  928.6 2.7 copy.16
  (15 shorter events, 0.1 us)
Async XLA Ops:
  7.2 405.3 %copy-start = (bf16[1,1,1,64,128,128]{5,4,3,2,1,0:T(8,128)(2,1)S(1)}, bf16[1,1,1,64,128,128]{5,4,3,2,1,0:T(8,128)(2,1)}, u32[]{:S(2)}) copy-start(bf16[1,1,1,64,128,128]{5,4,3,2,1,0:T(8,128)(2,1)} %param.12) | copy-start | bytes 6291460
  12.5 19.8 %copy-start.4 = (s32[1,1,1,3,64]{4,2,3,1,0:T(1,128)S(1)}, s32[1,1,1,3,64]{4,2,3,1,0:T(1,128)}, u32[]{:S(2)}) copy-start(s32[1,1,1,3,64]{4,2,3,1,0:T(1,128)} %param.10) | copy-start | bytes 2308
  12.5 19.9 %copy-start.5 = (s32[1,1,1,64]{3,2,1,0:T(1,128)S(1)}, s32[1,1,1,64]{3,2,1,0:T(1,128)}, u32[]{:S(2)}) copy-start(s32[1,1,1,64]{3,2,1,0:T(1,128)} %param.9) | copy-start | bytes 772
  12.5 388.9 %all-to-all-start = ((bf16[64,256,256]{2,1,0:T(8,128)(2,1)}), bf16[64,256,256]{2,1,0:T(8,128)(2,1)}, u32[]{:S(2)}, u32[]{:S(2)}) async-start(bf16[64,256,256]{2,1,0:T(8,128)(2,1)} %stack.2), calls=%async_computation | async-start | bytes 16777216 | tf_op jit(solution)/shard_map/all_to_all | solution.py:18
  31.6 444.8 %reduce-scatter.2.cloned.1.call-start = ((), (), s32[]{:S(2)}) async-start(), calls=%async_computation.2 | async-start | bytes 2359296 | tf_op jit(solution)/shard_map/reduce_scatter | solution.py:46
  436.9 6.3 copy-start.3
  440.6 2.7 copy-start.1
  443.2 33.2 %copy-start.2 = (bf16[256,256]{1,0:T(8,128)(2,1)S(1)}, bf16[256,256]{1,0:T(8,128)(2,1)}, u32[]{:S(2)}) copy-start(bf16[256,256]{1,0:T(8,128)(2,1)} %param.13) | copy-start | bytes 393220
  446.5 64.4 %all-gather.2.cloned.1.call-start = ((), (), s32[]{:S(2)}) async-start(), calls=%async_computation.3 | async-start | bytes 1179648 | tf_op jit(solution)/shard_map/all_gather | solution.py:54
  478.2 450.4 %all-reduce.2.cloned.1.call-start = ((), (), s32[]{:S(2)}) async-start(), calls=%async_computation.4 | async-start | bytes 3145728 | tf_op jit(solution)/shard_map/psum | solution.py:58
Sparse Core Ops, SparseCore 0:
  446.6 29.7 reduce-scatter.1
  479.1 31.7 all-gather.1
  517.1 411.4 all-reduce.1
